TPU v7x, 256 devices: a whole 4x4x8 slice. The times are simulated.
256 devices in a mesh: row: 8 (over x, y_hi), grp: 32 (over z, y_lo, core).
Axes of the slice: x: 4, y: 4 (y_hi: 2, y_lo: 2; y = y_hi * 2 + y_lo), z: 8, core: 2. Of those that a mesh axis runs over, the one named last changes fastest.
Arguments:
- segments: bfloat16 [32, 128, 128, 512], P('grp', 'row'), may hold values from -40 to 40
- conv_weight: bfloat16 [3, 512, 512], replicated, may hold values from -0.15625 to 0.15625
- gain: float32 [512], replicated, may hold values from 0.1 to 1.9
- head: bfloat16 [512, 128], replicated, may hold values from -0.25 to 0.25
- group: int32 [32, 128], P('grp', 'row'), may hold values from 0 to 7
- positive: int32 [32, 128], P('grp', 'row'), may hold values from 0 to 127, as said below
Outputs:
- grad_conv: float32 [3, 512, 512], replicated
- grad_gain: float32 [512], replicated
- projector_derivative: float32 [512, 128], replicated
Inputs may be any that keep to these rules, and one draw needn't show every extreme that they name: positive[c, i] is another segment of the same index c with the same group, and positive[c, positive[c, i]] == i.
All inputs are finite; a program needn't handle non-finite values.
Results may differ from a plain program's by a relative error of at most 0.003.
The roundings to bfloat16 on the way count: a program that leaves them out, or rounds other values in their place, can miss the bound.
Values sent between devices are 32-bit elements; how exact they have to be, the bound alone decides.
No kernel may reach another device: no remote copies, remote signals or barrier semaphores. Data moves between devices by JAX's collectives and lax.ppermute only.
A program may use at most 64 MiB of HBM per device.

v0:
```python
from functools import partial
import jax
import jax.numpy as jnp
from jax import lax
from jax.sharding import PartitionSpec as P

DILATION_GAP = 2
logit_divisor = 0.1


def unit_rows(values):
    return values * lax.rsqrt(jnp.mean(values * values, axis=-1, keepdims=True) + 1e-05)


def scale_embed(projected):
    return unit_rows(projected) * projected.shape[-1] ** (-0.5)


def filter_tap_window(normalized_rows, filter_tap_index, spacing):
    sequence_length = normalized_rows.shape[1]
    padded = jnp.pad(normalized_rows, ((0, 0), (spacing, spacing), (0, 0)))
    return padded[:, filter_tap_index * spacing : filter_tap_index * spacing + sequence_length]


def reverse_tap_gather(term, filter_tap_index, spacing):
    sequence_length = term.shape[1]
    padded = jnp.pad(term, ((0, 0), (spacing, spacing), (0, 0)))
    begin = (2 - filter_tap_index) * spacing
    return padded[:, begin : begin + sequence_length]


def encode(patient_piece_records, conv_weight, gain, head):
    inputs = patient_piece_records.astype(jnp.float32)
    unit = unit_rows(inputs)
    normalized_rows = (unit * gain).astype(jnp.bfloat16)
    segment_count, sequence_length, channel_count = normalized_rows.shape
    conv = jnp.zeros((segment_count * sequence_length, channel_count), jnp.float32)
    for filter_tap_index in range(conv_weight.shape[0]):
        shifted_input = filter_tap_window(normalized_rows, filter_tap_index, DILATION_GAP).reshape(
            segment_count * sequence_length, channel_count
        )
        conv = conv + jnp.dot(
            shifted_input, conv_weight[filter_tap_index], preferred_element_type=jnp.float32
        )
    conv = conv.reshape(segment_count, sequence_length, channel_count)
    hidden = inputs + jax.nn.gelu(conv, approximate=True)
    pooled = jnp.mean(hidden, axis=1).astype(jnp.bfloat16)
    projected = jnp.dot(pooled, head, preferred_element_type=jnp.float32)
    return (unit, normalized_rows, conv, pooled, projected)


def backward(embed_grad, unit, normalized_rows, conv, pooled, projected, conv_weight, head):
    projected_grad = jax.vjp(scale_embed, projected)[1](embed_grad)[0]
    projector_derivative = jnp.dot(
        pooled.astype(jnp.float32).T, projected_grad, precision=lax.Precision.HIGHEST
    )
    pooled_grad = jnp.dot(
        projected_grad, head.astype(jnp.float32).T, precision=lax.Precision.HIGHEST
    )
    segment_count, sequence_length, channel_count = conv.shape
    hidden_grad = jnp.broadcast_to(pooled_grad[:, None, :] / sequence_length, conv.shape)
    conv_grad = jax.vjp(partial(jax.nn.gelu, approximate=True), conv)[1](hidden_grad)[0].astype(
        jnp.bfloat16
    )
    flat_grad = conv_grad.reshape(segment_count * sequence_length, channel_count)
    tap_grads = []
    normalized_gradient = jnp.zeros((segment_count, sequence_length, channel_count), jnp.float32)
    for filter_tap_index in range(conv_weight.shape[0]):
        shifted_input = filter_tap_window(normalized_rows, filter_tap_index, DILATION_GAP).reshape(
            segment_count * sequence_length, channel_count
        )
        tap_grads.append(
            lax.dot_general(
                shifted_input,
                flat_grad,
                (((0,), (0,)), ((), ())),
                preferred_element_type=jnp.float32,
            )
        )
        backward_term = lax.dot_general(
            flat_grad,
            conv_weight[filter_tap_index],
            (((1,), (1,)), ((), ())),
            preferred_element_type=jnp.float32,
        )
        normalized_gradient = normalized_gradient + reverse_tap_gather(
            backward_term.reshape(segment_count, sequence_length, channel_count),
            filter_tap_index,
            DILATION_GAP,
        )
    grad_conv = jnp.stack(tap_grads)
    grad_gain = jnp.sum(normalized_gradient * unit, axis=(0, 1))
    return (grad_conv, grad_gain, projector_derivative)


def body(segments, conv_weight, gain, head, group, positive):
    patient_piece_records = segments[0]
    group_ids = group[0]
    partners = positive[0]
    unit, normalized_rows, conv, pooled, projected = encode(
        patient_piece_records, conv_weight, gain, head
    )
    encounter_latent_vector = scale_embed(projected)
    gathered_embedding, all_groups = (
        lax.all_gather(encounter_latent_vector, "row", axis=0, tiled=True),
        lax.all_gather(group_ids, "row", axis=0, tiled=True),
    )
    local_count = encounter_latent_vector.shape[0]
    matrix_height_number = gathered_embedding.shape[0]
    global_multiplier = (matrix_height_number * lax.axis_size("grp")) ** (-0.5) / logit_divisor
    own_rows = lax.axis_index("row") * local_count + jnp.arange(local_count, dtype=jnp.int32)
    columns = jnp.arange(matrix_height_number, dtype=jnp.int32)
    cosine_affinity_matrix = (
        jnp.dot(encounter_latent_vector, gathered_embedding.T, precision=lax.Precision.HIGHEST)
        / logit_divisor
    )
    same_group = (group_ids[:, None] == all_groups[None, :]) & (
        own_rows[:, None] != columns[None, :]
    )
    log_total = jnp.log(
        jnp.sum(jnp.where(same_group, jnp.exp(cosine_affinity_matrix), 0.0), axis=1)
    )
    softmax = jnp.where(same_group, jnp.exp(cosine_affinity_matrix - log_total[:, None]), 0.0)
    row_term = jnp.dot(softmax, gathered_embedding, precision=lax.Precision.HIGHEST)
    partner_pick = (partners[:, None] == columns[None, :]).astype(jnp.float32)
    partner_embed = jnp.dot(partner_pick, gathered_embedding, precision=lax.Precision.HIGHEST)
    column_term = lax.psum_scatter(
        lax.dot_general(
            softmax,
            encounter_latent_vector,
            (((0,), (0,)), ((), ())),
            precision=lax.Precision.HIGHEST,
            preferred_element_type=jnp.float32,
        ),
        "row",
        scatter_dimension=0,
        tiled=True,
    )
    embed_grad = global_multiplier * (row_term + column_term - 2.0 * partner_embed)
    grads = backward(embed_grad, unit, normalized_rows, conv, pooled, projected, conv_weight, head)
    grads = lax.psum((grads[0], grads[1], grads[2]), ("row", "grp"))
    return (grads[0], grads[1], grads[2])


def solution(mesh):
    placed = (P("grp", "row", None, None), P(), P(), P(), P("grp", "row"), P("grp", "row"))
    return jax.shard_map(
        body, mesh=mesh, in_specs=placed, out_specs=(P(), P(), P()), check_vma=False
    )
```

profile of v0, /device:TPU:2, one launch (start us, length us, event | category | flops | bytes accessed | tf_op | source)
XLA Modules:
  0.0 477.1 jit_solution(5161826225677553854)
XLA Ops:
  7.2 3.0 copy.23
  10.7 0.7 fusion.5
  11.4 2.1 fusion.10
  13.5 3.2 pad_slice_fusion.2
  16.7 3.9 copy.24
  20.6 3.9 copy.25
  24.6 5.0 %fusion.45 = f32[2048,512]{1,0:T(8,128)} fusion(bf16[2048,512]{1,0:T(8,128)(2,1)} %bitcast.96, bf16[3,512,512]{2,1,0:T(8,128)(2,1)} %param.7), kind=kOutput, calls=%fused_computation.63 | convolution fusion | flops 1073741824 | bytes 6815744 | tf_op jit(solution)/shard_map/dot_general | solution.py:42
  29.6 4.3 fusion.43
  33.9 3.9 copy.26
  37.8 7.4 %add_add_fusion = f32[2048,512]{1,0:T(8,128)} fusion(f32[2048,512]{1,0:T(8,128)} %fusion.45, f32[2048,512]{1,0:T(8,128)} %fusion.43, bf16[2048,512]{1,0:T(8,128)(2,1)} %bitcast.98, bf16[3,512,512]{2,1,0:T(8,128)(2,1)} %param.7), kind=kOutput, calls=%fused_computation.44 | convolution fusion | flops 1075838976 | bytes 15204352 | tf_op jit(solution)/shard_map/dot_general | solution.py:42
  45.2 5.3 %copy.30 = f32[16,128,512]{1,2,0:T(8,128)} copy(f32[16,128,512]{2,1,0:T(8,128)} %bitcast.91) | data formatting | bytes 8388608 | tf_op jit(solution)/shard_map/reshape | solution.py:45
  50.5 3.4 fusion.8
  54.2 0.6 dynamic-slice
  55.6 11.9 %all-reduce.3 = s32[128]{0:T(128)S(1)} all-reduce(s32[128]{0:T(128)S(1)} %bitcast_dynamic-update-slice_fusion), channel_id=2, replica_groups=mesh['row'=8,'grp'=32] {'row'}, use_global_device_ids=true, to_apply=%add.3 | all-reduce | flops 128 | bytes 1024
  67.6 33.3 %all_gather.7 = f32[128,128]{1,0:T(8,128)S(1)} all-gather(f32[16,128]{1,0:T(8,128)S(1)} %multiply_multiply_fusion.4), channel_id=1, replica_groups=mesh['row'=8,'grp'=32] {'row'}, dimensions={0}, use_global_device_ids=true | all-gather | bytes 73728 | tf_op jit(solution)/shard_map/all_gather | solution.py:105
  101.3 1.0 fusion.56
  102.5 78.2 %reduce-scatter.2.cloned.1.call-done = f32[16,128]{1,0:T(8,128)} async-done(((f32[128,128]{1,0:T(8,128)}), f32[16,128]{1,0:T(8,128)}) %reduce-scatter.2.cloned.1.call-update) | async-done | bytes 8208 | tf_op jit(solution)/shard_map/reduce_scatter | solution.py:127
  180.7 1.1 convolution_add_fusion
  182.4 6.5 %fusion.17 = bf16[16,128,512]{1,2,0:T(8,128)(2,1)S(1)} fusion(f32[16,128,512]{1,2,0:T(8,128)} %copy.30, f32[16,512]{1,0:T(8,128)S(1)} %get-tuple-element.8, f32[16,512]{1,0:T(8,128)S(1)} %get-tuple-element.7), kind=kLoop, calls=%fused_computation.27 | loop fusion | flops 19922944 | bytes 6356992 | tf_op jit(solution)/shard_map/convert_element_type | solution.py:62
  188.9 2.7 fusion.24
  191.6 1.3 convolution_bitcast_fusion
  192.9 1.3 convolution_bitcast_fusion.1
  194.2 1.0 fusion.54
  195.2 1.2 fusion.33
  196.5 2.0 pad_maximum_fusion
  198.5 3.1 fusion.40
  201.6 1.3 fusion.37
  202.9 2.6 fusion.6
  205.5 75.3 %psum.22 = f32[512]{0:T(512)} all-reduce(f32[512]{0:T(512)S(1)} %fusion.6), channel_id=1, replica_groups=mesh['row'=8,'grp'=32] {'row','grp'}, use_global_device_ids=true, to_apply=%region_8.9 | all-reduce | flops 512 | bytes 4096 | tf_op jit(solution)/shard_map/psum | solution.py:141
  280.8 184.9 %all-reduce.7.cloned.1.call-done = (f32[3,512,512]{2,1,0:T(8,128)}, f32[512,128]{1,0:T(8,128)}) async-done(((f32[3,512,512]{2,1,0:T(8,128)}, f32[512,128]{1,0:T(8,128)}), (f32[3,512,512]{2,1,0:T(8,128)}, f32[512,128]{1,0:T(8,128)})) %all-reduce.7.cloned.1.call-update) | async-done | bytes 3407888 | tf_op jit(solution)/shard_map/psum | solution.py:141
  465.7 3.9 copy.50
  469.6 0.7 copy.51
  (45 shorter events, 2.1 us)
Async XLA Ops:
  7.2 46.8 %copy-start = (bf16[512,128]{1,0:T(8,128)(2,1)S(1)}, bf16[512,128]{1,0:T(8,128)(2,1)}, u32[]{:S(2)}) copy-start(bf16[512,128]{1,0:T(8,128)(2,1)} %param.9) | copy-start | bytes 393220
  7.2 3.5 copy-start.10
  7.2 173.5 %reduce-scatter.2.cloned.1.call-start = ((), (), s32[]{:S(2)}) async-start(), calls=%async_computation.1 | async-start | bytes 73728 | tf_op jit(solution)/shard_map/reduce_scatter | solution.py:127
  11.4 5.3 %copy-start.5 = (bf16[16,128,512]{1,2,0:T(8,128)(2,1)}, bf16[16,128,512]{1,2,0:T(8,128)(2,1)S(1)}, u32[]{:S(2)}) copy-start(bf16[16,128,512]{1,2,0:T(8,128)(2,1)S(1)} %fusion.5) | copy-start | bytes 6291460
  24.6 5.0 %copy-start.4 = (bf16[1,16,128,512]{3,2,1,0:T(8,128)(2,1)S(1)}, bf16[1,16,128,512]{3,2,1,0:T(8,128)(2,1)}, u32[]{:S(2)}) copy-start(bf16[1,16,128,512]{3,2,1,0:T(8,128)(2,1)} %copy.25) | copy-start | bytes 6291460
  50.5 3.7 copy-start.13
  50.5 5.0 %copy-start.12 = (s32[1,16]{1,0:T(1,128)S(1)}, s32[1,16]{1,0:T(1,128)}, u32[]{:S(2)}) copy-start(s32[1,16]{1,0:T(1,128)} %param.10) | copy-start | bytes 196
  50.5 131.3 %copy-start.11 = (s32[1,16]{1,0:T(1,128)S(1)}, s32[1,16]{1,0:T(1,128)}, u32[]{:S(2)}) copy-start(s32[1,16]{1,0:T(1,128)} %param.11) | copy-start | bytes 196
  102.3 363.4 %all-reduce.7.cloned.1.call-start = ((), (), s32[]{:S(2)}) async-start(), calls=%async_computation.2 | async-start | bytes 6815744 | tf_op jit(solution)/shard_map/psum | solution.py:141
  180.7 8.1 %copy-start.1 = (f32[2048,512]{1,0:T(8,128)S(1)}, f32[2048,512]{1,0:T(8,128)}, u32[]{:S(2)}) copy-start(f32[2048,512]{1,0:T(8,128)} %add_add_fusion) | copy-start | bytes 12582916
  188.8 2.7 copy-start.6
  191.6 3.7 copy-start.2
  192.9 2.4 copy-start.7
  198.5 3.1 copy-start.3
  198.5 3.1 copy-start.8
  465.7 3.9 copy-start.9
Sparse Core Ops, SparseCore 0:
  102.4 78.2 reduce-scatter.1
  198.6 267.0 all-reduce.6
where the time goes:
time: 478 us; the launch traced here: 477 us
  waiting for transfers between devices  263 us (55%)
  blocking collectives  121 us (25%)
  matrix products  31.8 us (7%)
  local copies, waits for them, and re-layouts  28.6 us (6%)
  other arithmetic  17.9 us (4%)
  between operations  15 us (3%)
    psum x1, waiting for transfers between devices, body(): grads = lax.psum((grads[0], grads[1], grads[2]), ('row', 'grp'))  185 us
    reduce_scatter x1, waiting for transfers between devices, body(): lax.psum_scatter(lax.dot_general(softmax, encounter_latent_vector, (((0,)...  78.2 us
    psum x1, blocking collectives, body(): grads = lax.psum((grads[0], grads[1], grads[2]), ('row', 'grp'))  75.3 us
    all_gather x1, blocking collectives, body(): lax.all_gather(encounter_latent_vector, 'row', axis=0, tiled=True)  33.3 us
    dot_general x3, matrix products, encode(): jnp.dot(shifted_input, conv_weight[filter_tap_index], preferred_element_t...  16.7 us
    unnamed x1, blocking collectives  11.9 us
    slice x3, local copies, waits for them, and re-layouts, filter_tap_window(): padded[:, filter_tap_index * spacing:filter_tap_index * spacing + sequenc...  11 us
  transfers between devices with their start and end apart: 2, of which 2 were waited for; matrix products, arithmetic and copies ran while one was open for 1% of the time, Pallas kernels for 0%

commit v1 on v0

--- a/solution.py
+++ b/solution.py
@@ -6,6 +6,13 @@
 
 DILATION_GAP = 2
 logit_divisor = 0.1
+
+
+def gather_over(shard, name, d):
+    peers = lax.axis_size(name)
+    shards = jnp.stack([shard for _ in range(peers)])
+    shards = lax.all_to_all(shards, name, split_axis=0, concat_axis=0)
+    return jnp.concatenate(shards, axis=d)
 
 
 def unit_rows(values):
@@ -102,7 +109,7 @@
     )
     encounter_latent_vector = scale_embed(projected)
     gathered_embedding, all_groups = (
-        lax.all_gather(encounter_latent_vector, "row", axis=0, tiled=True),
+        gather_over(encounter_latent_vector, "row", 0),
         lax.all_gather(group_ids, "row", axis=0, tiled=True),
     )
     local_count = encounter_latent_vector.shape[0]

time: 478 us -> 452 us (0.946)
  blocking collectives: 121 us -> 87.1 us
  starting transfers between devices: 0.26 us -> 7.69 us
    all_gather x1 -> x0, blocking collectives: 33.3 us -> none  [body(): lax.all_gather(encounter_latent_vector, 'row', axis=0, tiled=True)]
    all_to_all x0 -> x1, starting transfers between devices: none -> 7.46 us  [gather_over(): shards = lax.all_to_all(shards, name, split_axis=0, concat_axis=0)]
  transfers between devices with their start and end apart: 2 -> 3, of which waited for: 2 -> 2; matrix products, arithmetic and copies ran while one was open for 1% -> 2% of each run, Pallas kernels for 0% -> 0%
where the time goes in v1:
time: 452 us; the launch traced here: 451 us
  waiting for transfers between devices  262 us (58%)
  blocking collectives  87.1 us (19%)
  matrix products  31.8 us (7%)
  local copies, waits for them, and re-layouts  29.3 us (6%)
  other arithmetic  17.9 us (4%)
  between operations  14.9 us (3%)
  starting transfers between devices  7.69 us (2%)
    psum x1, waiting for transfers between devices, body(): grads = lax.psum((grads[0], grads[1], grads[2]), ('row', 'grp'))  185 us
    reduce_scatter x1, waiting for transfers between devices, body(): lax.psum_scatter(lax.dot_general(softmax, encounter_latent_vector, (((0,)...  77.4 us
    psum x1, blocking collectives, body(): grads = lax.psum((grads[0], grads[1], grads[2]), ('row', 'grp'))  75.3 us
    dot_general x3, matrix products, encode(): jnp.dot(shifted_input, conv_weight[filter_tap_index], preferred_element_t...  16.7 us
    unnamed x1, blocking collectives  11.9 us
    slice x3, local copies, waits for them, and re-layouts, filter_tap_window(): padded[:, filter_tap_index * spacing:filter_tap_index * spacing + sequenc...  11 us
    convert_element_type x2, other arithmetic, backward(): jax.vjp(partial(jax.nn.gelu, approximate=True), conv)[1](hidden_grad)[0]  9.15 us
  transfers between devices with their start and end apart: 3, of which 2 were waited for; matrix products, arithmetic and copies ran while one was open for 2% of the time, Pallas kernels for 0%

profile of v1, /device:TPU:2, one launch (start us, length us, event | category | flops | bytes accessed | tf_op | source)
XLA Modules:
  0.0 451.0 jit_solution(11084042266883020221)
XLA Ops:
  7.2 3.1 copy.23
  10.7 0.7 fusion.5
  11.4 2.1 fusion.10
  13.5 3.2 pad_slice_fusion.2
  16.7 3.9 copy.24
  20.6 3.9 copy.25
  24.6 5.0 %fusion.45 = f32[2048,512]{1,0:T(8,128)} fusion(bf16[2048,512]{1,0:T(8,128)(2,1)} %bitcast.97, bf16[3,512,512]{2,1,0:T(8,128)(2,1)} %param.7), kind=kOutput, calls=%fused_computation.63 | convolution fusion | flops 1073741824 | bytes 6815744 | tf_op jit(solution)/shard_map/dot_general | solution.py:49
  29.6 4.3 fusion.43
  33.9 3.9 copy.26
  37.8 7.4 %add_add_fusion = f32[2048,512]{1,0:T(8,128)} fusion(f32[2048,512]{1,0:T(8,128)} %fusion.45, f32[2048,512]{1,0:T(8,128)} %fusion.43, bf16[2048,512]{1,0:T(8,128)(2,1)} %bitcast.99, bf16[3,512,512]{2,1,0:T(8,128)(2,1)} %param.7), kind=kOutput, calls=%fused_computation.44 | convolution fusion | flops 1075838976 | bytes 15204352 | tf_op jit(solution)/shard_map/dot_general | solution.py:49
  45.2 5.3 %copy.30 = f32[16,128,512]{1,2,0:T(8,128)} copy(f32[16,128,512]{2,1,0:T(8,128)} %bitcast.92) | data formatting | bytes 8388608 | tf_op jit(solution)/shard_map/reshape | solution.py:52
  50.5 3.4 fusion.8
  54.3 0.6 stack.10
  55.0 7.5 %all-to-all-start = ((f32[8,16,128]{2,1,0:T(8,128)}), f32[8,16,128]{2,1,0:T(8,128)S(1)}, u32[]{:S(2)}, u32[]{:S(2)}) async-start(f32[8,16,128]{2,1,0:T(8,128)} %stack.10), calls=%async_computation | async-start | bytes 131072 | tf_op jit(solution)/shard_map/all_to_all | solution.py:14
  63.8 11.9 %all-reduce.3 = s32[128]{0:T(128)S(1)} all-reduce(s32[128]{0:T(128)S(1)} %bitcast_dynamic-update-slice_fusion), channel_id=2, replica_groups=mesh['row'=8,'grp'=32] {'row'}, use_global_device_ids=true, to_apply=%add.3 | all-reduce | flops 128 | bytes 1024
  76.0 1.0 fusion.56
  77.3 77.4 %reduce-scatter.2.cloned.1.call-done = f32[16,128]{1,0:T(8,128)} async-done(((f32[128,128]{1,0:T(8,128)}), f32[16,128]{1,0:T(8,128)}) %reduce-scatter.2.cloned.1.call-update) | async-done | bytes 8208 | tf_op jit(solution)/shard_map/reduce_scatter | solution.py:134
  154.7 1.1 convolution_add_fusion
  156.4 6.5 %fusion.17 = bf16[16,128,512]{1,2,0:T(8,128)(2,1)S(1)} fusion(f32[16,128,512]{1,2,0:T(8,128)} %copy.30, f32[16,512]{1,0:T(8,128)S(1)} %get-tuple-element.8, f32[16,512]{1,0:T(8,128)S(1)} %get-tuple-element.7), kind=kLoop, calls=%fused_computation.27 | loop fusion | flops 19922944 | bytes 6356992 | tf_op jit(solution)/shard_map/convert_element_type | solution.py:69
  162.8 2.7 fusion.24
  165.6 1.3 convolution_bitcast_fusion
  166.9 1.3 convolution_bitcast_fusion.1
  168.2 1.0 fusion.54
  169.2 1.2 fusion.33
  170.5 2.0 pad_maximum_fusion
  172.5 3.1 fusion.40
  175.6 1.3 fusion.37
  176.9 2.6 fusion.6
  179.5 75.3 %psum.22 = f32[512]{0:T(512)} all-reduce(f32[512]{0:T(512)S(1)} %fusion.6), channel_id=1, replica_groups=mesh['row'=8,'grp'=32] {'row','grp'}, use_global_device_ids=true, to_apply=%region_8.9 | all-reduce | flops 512 | bytes 4096 | tf_op jit(solution)/shard_map/psum | solution.py:148
  254.7 184.8 %all-reduce.7.cloned.1.call-done = (f32[3,512,512]{2,1,0:T(8,128)}, f32[512,128]{1,0:T(8,128)}) async-done(((f32[3,512,512]{2,1,0:T(8,128)}, f32[512,128]{1,0:T(8,128)}), (f32[3,512,512]{2,1,0:T(8,128)}, f32[512,128]{1,0:T(8,128)})) %all-reduce.7.cloned.1.call-update) | async-done | bytes 3407888 | tf_op jit(solution)/shard_map/psum | solution.py:148
  439.6 3.9 copy.50
  443.5 0.7 copy.51
  (47 shorter events, 2.7 us)
Async XLA Ops:
  7.2 46.8 %copy-start = (bf16[512,128]{1,0:T(8,128)(2,1)S(1)}, bf16[512,128]{1,0:T(8,128)(2,1)}, u32[]{:S(2)}) copy-start(bf16[512,128]{1,0:T(8,128)(2,1)} %param.9) | copy-start | bytes 393220
  7.2 3.5 copy-start.10
  11.4 5.3 %copy-start.5 = (bf16[16,128,512]{1,2,0:T(8,128)(2,1)}, bf16[16,128,512]{1,2,0:T(8,128)(2,1)S(1)}, u32[]{:S(2)}) copy-start(bf16[16,128,512]{1,2,0:T(8,128)(2,1)S(1)} %fusion.5) | copy-start | bytes 6291460
  24.6 5.0 %copy-start.4 = (bf16[1,16,128,512]{3,2,1,0:T(8,128)(2,1)S(1)}, bf16[1,16,128,512]{3,2,1,0:T(8,128)(2,1)}, u32[]{:S(2)}) copy-start(bf16[1,16,128,512]{3,2,1,0:T(8,128)(2,1)} %copy.25) | copy-start | bytes 6291460
  50.5 11.9 %copy-start.13 = (u32[256]{0:T(256)S(1)}, u32[256]{0:T(256)}, u32[]{:S(2)}) copy-start(u32[256]{0:T(256)} %constant.65) | copy-start | bytes 3076
  50.5 13.2 %copy-start.12 = (s32[1,16]{1,0:T(1,128)S(1)}, s32[1,16]{1,0:T(1,128)}, u32[]{:S(2)}) copy-start(s32[1,16]{1,0:T(1,128)} %param.10) | copy-start | bytes 196
  50.5 105.2 %copy-start.11 = (s32[1,16]{1,0:T(1,128)S(1)}, s32[1,16]{1,0:T(1,128)}, u32[]{:S(2)}) copy-start(s32[1,16]{1,0:T(1,128)} %param.11) | copy-start | bytes 196
  55.0 20.7 %all-to-all-start = ((f32[8,16,128]{2,1,0:T(8,128)}), f32[8,16,128]{2,1,0:T(8,128)S(1)}, u32[]{:S(2)}, u32[]{:S(2)}) async-start(f32[8,16,128]{2,1,0:T(8,128)} %stack.10), calls=%async_computation | async-start | bytes 131072 | tf_op jit(solution)/shard_map/all_to_all | solution.py:14
  62.4 92.2 %reduce-scatter.2.cloned.1.call-start = ((), (), s32[]{:S(2)}) async-start(), calls=%async_computation.2 | async-start | bytes 73728 | tf_op jit(solution)/shard_map/reduce_scatter | solution.py:134
  77.1 362.5 %all-reduce.7.cloned.1.call-start = ((), (), s32[]{:S(2)}) async-start(), calls=%async_computation.3 | async-start | bytes 6815744 | tf_op jit(solution)/shard_map/psum | solution.py:148
  154.7 8.1 %copy-start.1 = (f32[2048,512]{1,0:T(8,128)S(1)}, f32[2048,512]{1,0:T(8,128)}, u32[]{:S(2)}) copy-start(f32[2048,512]{1,0:T(8,128)} %add_add_fusion) | copy-start | bytes 12582916
  162.8 2.7 copy-start.6
  165.6 3.7 copy-start.2
  166.9 2.3 copy-start.7
  172.4 3.1 copy-start.3
  172.5 3.1 copy-start.8
  439.6 3.9 copy-start.9
Sparse Core Ops, SparseCore 0:
  77.2 77.4 reduce-scatter.1
  172.6 266.9 all-reduce.6
